TPU v7x, 256 devices: a whole 4x4x8 slice. The times are simulated.
256 devices in a mesh: win: 32 (over y, x, core), grp: 8 (over z).
Axes of the slice: x: 4, y: 4, z: 8, core: 2. Of those that a mesh axis runs over, the one named last changes fastest.
Arguments:
- traces: bfloat16 [256, 512, 2048], P(('win', 'grp'))
- pair_lists: int32 [32, 3], P('win'), may hold values from -1 to 3, as said below
- observed: float32 [32, 3, 16, 16, 2048], P('win'), may hold values from -4 to 4
Outputs:
- correl: float32 [32, 3, 16, 16, 2048], P('win', None, None, None, 'grp')
- trace_gradient: bfloat16 [256, 512, 2048], P(('win', 'grp'))
Inputs may be any that keep to these rules, and one draw needn't show every extreme that they name: `pair_lists`: each row lists distinct offsets in increasing order, followed by -1 in its empty slots; block a lists only offsets o with a + o < 32; every block lists at least one offset, and block 0 fills all 3 slots and lists offset 4 - 1.
All inputs are finite; a program needn't handle non-finite values.
Results may differ from a plain program's by a relative error of at most 0.014.
Values may be sent and summed in bfloat16 or wider, within the bound.
No kernel may reach another device: no remote copies, remote signals or barrier semaphores. Data moves between devices by JAX's collectives and lax.ppermute only.
A program may use at most 192 MiB of HBM per device.

v0:
```python
import math
import jax
import jax.numpy as jnp
from jax import lax
from jax.sharding import PartitionSpec as P

SEG = 2048
FREQ = 1024
BAND = 64
OFFSETS = 4


def passed_along(array, axis, by):
    peers = lax.axis_size(axis)
    pairs = [(i, i + by) for i in range(peers) if 0 <= i + by < peers]
    return lax.ppermute(array, axis, pairs)


def dft_table(first_column, column_count):
    samples = jnp.arange(SEG, dtype=jnp.int32)
    columns = first_column + jnp.arange(column_count, dtype=jnp.int32)
    harmonic = columns % FREQ
    phases = samples[:, None] * harmonic[None, :] % SEG
    angles = phases.astype(jnp.float32) * (2.0 * math.pi / SEG)
    values = jnp.where(columns[None, :] < FREQ, jnp.cos(angles), -jnp.sin(angles))
    return values.astype(jnp.bfloat16)


def whiten(spectrum):
    halfway = spectrum.shape[-1] // 2
    real_part = spectrum[..., :halfway]
    imag_part = spectrum[..., halfway:]
    power_bins = real_part * real_part + imag_part * imag_part
    banded = power_bins.reshape(power_bins.shape[:-1] + (halfway // BAND, BAND))
    inverse = lax.rsqrt(jnp.mean(banded, axis=-1) + 1e-05)
    spread = jnp.broadcast_to(inverse[..., None], banded.shape).reshape(power_bins.shape)
    return spectrum * jnp.concatenate([spread, spread], axis=-1)


def split_halves(operand):
    halfway = operand.shape[-1] // 2
    return (operand[..., :halfway], operand[..., halfway:])


def widen(operand):
    return operand.astype(jnp.float32)


def correlate(leading, trailing, windows_total):
    lead_real, lead_imag = split_halves(leading)
    trail_real, trail_imag = split_halves(trailing)
    left_real = widen(lead_real)[:, :, None, :]
    left_imag = widen(lead_imag)[:, :, None, :]
    right_real = widen(trail_real)[:, None, :, :]
    right_imag = widen(trail_imag)[:, None, :, :]
    real_sum = jnp.sum(left_real * right_real + left_imag * right_imag, axis=0)
    imag_sum = jnp.sum(left_real * right_imag - left_imag * right_real, axis=0)
    return jnp.concatenate([real_sum, imag_sum], axis=-1) / windows_total


def pull_first(residual, trailing):
    resid_real, resid_imag = split_halves(residual)
    trail_real, trail_imag = split_halves(trailing)
    left_real = widen(resid_real)[None]
    left_imag = widen(resid_imag)[None]
    right_real = widen(trail_real)[:, None, :, :]
    right_imag = widen(trail_imag)[:, None, :, :]
    real_part = jnp.sum(left_real * right_real + left_imag * right_imag, axis=2)
    imag_part = jnp.sum(left_real * right_imag - left_imag * right_real, axis=2)
    return jnp.concatenate([real_part, imag_part], axis=-1)


def pull_second(residual, leading):
    resid_real, resid_imag = split_halves(residual)
    lead_real, lead_imag = split_halves(leading)
    left_real = widen(resid_real)[None]
    left_imag = widen(resid_imag)[None]
    right_real = widen(lead_real)[:, :, None, :]
    right_imag = widen(lead_imag)[:, :, None, :]
    real_part = jnp.sum(left_real * right_real - left_imag * right_imag, axis=1)
    imag_part = jnp.sum(left_real * right_imag + left_imag * right_real, axis=1)
    return jnp.concatenate([real_part, imag_part], axis=-1)


def on_device(traces, pair_lists, observed):
    win_dev, channels, samples = traces.shape
    column_total = 2 * FREQ
    column_step = min(512, column_total)
    tables = [
        dft_table(start_col, column_step) for start_col in range(0, column_total, column_step)
    ]
    flat_traces = traces.reshape(win_dev * channels, samples)
    spectra = jnp.concatenate(
        [
            jnp.dot(flat_traces, table_part, preferred_element_type=jnp.float32)
            for table_part in tables
        ],
        axis=1,
    )
    spectra = spectra.reshape(win_dev, channels, column_total)
    whitened = whiten(spectra).astype(jnp.bfloat16)
    grp_count = lax.axis_size("grp")
    share_width = column_total // grp_count
    moved_blocks = lax.all_to_all(whitened, "win", split_axis=1, concat_axis=0, tiled=True)
    windows_total = moved_blocks.shape[0] * grp_count
    partner_list = [moved_blocks] + [
        passed_along(moved_blocks, "win", -offset) for offset in range(1, OFFSETS)
    ]
    stacked = jnp.stack(partner_list)
    offsets = pair_lists[0]
    slot_total = offsets.shape[0]
    live_slots = (offsets >= 0).astype(jnp.float32)[:, None, None, None]
    partners = [
        lax.dynamic_index_in_dim(stacked, jnp.maximum(offsets[slot_index], 0), 0, keepdims=False)
        for slot_index in range(slot_total)
    ]
    correl = (
        jnp.stack(
            [correlate(moved_blocks, partner_block, windows_total) for partner_block in partners]
        )
        * live_slots
    )
    share_start = lax.axis_index("grp") * share_width
    totals = lax.psum(correl, "grp")
    correl_share = lax.dynamic_slice_in_dim(totals, share_start, share_width, 3)
    residual = ((totals - observed[0]) * live_slots).astype(jnp.bfloat16)
    own_grad = pull_first(residual[0], partners[0])
    for slot_index in range(1, slot_total):
        own_grad = own_grad + pull_first(residual[slot_index], partners[slot_index])
    contrib = []
    for offset in range(OFFSETS):
        chosen = jnp.zeros_like(residual[0])
        for slot_index in range(slot_total):
            chosen = jnp.where(offsets[slot_index] == offset, residual[slot_index], chosen)
        contrib.append(pull_second(chosen, moved_blocks))
    white_grad = own_grad + contrib[0]
    for offset in range(1, OFFSETS):
        white_grad = white_grad + passed_along(
            contrib[offset].astype(jnp.bfloat16), "win", offset
        ).astype(jnp.float32)
    returned = lax.all_to_all(
        white_grad.astype(jnp.bfloat16), "win", split_axis=0, concat_axis=1, tiled=True
    )
    unused, pullback = jax.vjp(whiten, spectra)
    spectra_grad = pullback(returned.astype(jnp.float32))[0].astype(jnp.bfloat16)
    flat_grad = spectra_grad.reshape(win_dev * channels, column_total)
    trace_grad = jnp.zeros((win_dev * channels, samples), jnp.float32)
    for table_index in range(len(tables)):
        start_col = table_index * column_step
        trace_grad = trace_grad + jnp.dot(
            flat_grad[:, start_col : start_col + column_step],
            tables[table_index].T,
            preferred_element_type=jnp.float32,
        )
    return (correl_share[None], trace_grad.reshape(win_dev, channels, samples).astype(jnp.bfloat16))


def solution(mesh):
    return jax.shard_map(
        on_device,
        mesh=mesh,
        in_specs=(P(("win", "grp"), None, None), P("win", None), P("win", None, None, None, None)),
        out_specs=(P("win", None, None, None, "grp"), P(("win", "grp"), None, None)),
        check_vma=False,
    )
```

profile of v0, /device:TPU:1, one launch (start us, length us, event | category | flops | bytes accessed | tf_op | source)
XLA Modules:
  0.0 817.0 jit_solution(5095351248463171921)
XLA Ops:
  7.3 1.4 copy-done
  8.8 17.5 %fusion.41 = f32[512,512]{1,0:T(8,128)S(1)} fusion(bf16[1,512,2048]{2,1,0:T(8,128)(2,1)S(1)} %copy-done, s32[512]{0:T(512)S(1)} %add_select_fusion.4, pred[512]{0:T(512)(128)(4,1)S(1)} %fusion.60), kind=kOutput, calls=%fused_computation.95 | convolution fusion | flops 1091567616 | bytes 3148288 | tf_op jit(solution)/shard_map/dot_general | solution.py:95
  26.2 17.2 %fusion.43 = f32[512,512]{1,0:T(8,128)S(1)} fusion(bf16[1,512,2048]{2,1,0:T(8,128)(2,1)S(1)} %copy-done, s32[512]{0:T(512)S(1)} %add_select_fusion.5, pred[512]{0:T(512)(128)(4,1)S(1)} %fusion.61), kind=kOutput, calls=%fused_computation.97 | convolution fusion | flops 1091567616 | bytes 3148288 | tf_op jit(solution)/shard_map/dot_general | solution.py:95
  43.4 17.6 %fusion.45 = f32[512,512]{1,0:T(8,128)S(1)} fusion(bf16[1,512,2048]{2,1,0:T(8,128)(2,1)S(1)} %copy-done, s32[512]{0:T(512)S(1)} %add_select_fusion.6, pred[512]{0:T(512)(128)(4,1)S(1)} %fusion.62), kind=kOutput, calls=%fused_computation.99 | convolution fusion | flops 1091567616 | bytes 3148288 | tf_op jit(solution)/shard_map/dot_general | solution.py:95
  61.0 17.2 %fusion.47 = f32[512,512]{1,0:T(8,128)S(1)} fusion(bf16[1,512,2048]{2,1,0:T(8,128)(2,1)S(1)} %copy-done, s32[512]{0:T(512)S(1)} %add_select_fusion.7, pred[512]{0:T(512)(128)(4,1)S(1)} %iota_compare_fusion), kind=kOutput, calls=%fused_computation.101 | convolution fusion | flops 1091567616 | bytes 3148288 | tf_op jit(solution)/shard_map/dot_general | solution.py:95
  79.2 2.0 copy-done.3
  82.7 3.9 fusion.16
  86.6 10.8 %copy.14 = bf16[1,512,2048]{2,0,1:T(2,128)(2,1)} copy(bf16[1,512,2048]{1,2,0:T(8,128)(2,1)} %fusion.16) | data formatting | bytes 4194304 | tf_op jit(solution)/shard_map/convert_element_type | solution.py:101
  98.0 13.2 %reduce.2 = bf16[512,2048]{1,0:T(8,128)(2,1)S(1)} reduce(bf16[512,1,2048]{2,1,0:T(2,128)(2,1)} %bitcast.118, bf16[]{:T(256)} %broadcast.306), dimensions={1}, to_apply=%bitcast.108.reduce_sub_computation | reduce | bytes 4194306
  111.1 2.8 reshape.499
  113.9 37.0 %all_to_all.21 = bf16[32,2,16384]{2,1,0:T(2,128)(2,1)S(1)} all-to-all(bf16[32,2,16384]{2,1,0:T(2,128)(2,1)} %reshape.499), channel_id=1, replica_groups=mesh['win'=32,'grp'=8] {'win'}, dimensions={0} | all-to-all | bytes 4194304 | tf_op jit(solution)/shard_map/all_to_all | solution.py:104
  150.9 6.8 reshape.500
  157.6 3.5 copy.17
  163.7 2.3 collective-permute-start
  168.5 2.5 slice_convert_fusion.7
  171.1 18.9 %collective-permute-done.2 = bf16[32,16,2048]{2,1,0:T(8,128)(2,1)S(1)} collective-permute-done((bf16[32,16,2048]{2,1,0:T(8,128)(2,1)S(1)}, bf16[32,16,2048]{2,1,0:T(8,128)(2,1)S(1)}, u32[]{:S(2)}, u32[]{:S(2)}) %collective-permute-start.2) | collective-permute-done | bytes 2097184 | tf_op jit(solution)/shard_map/ppermute | solution.py:16
  190.0 63.7 %collective-permute-done.1 = bf16[32,16,2048]{2,1,0:T(8,128)(2,1)S(1)} collective-permute-done((bf16[32,16,2048]{2,1,0:T(8,128)(2,1)S(1)}, bf16[32,16,2048]{2,1,0:T(8,128)(2,1)S(1)}, u32[]{:S(2)}, u32[]{:S(2)}) %collective-permute-start.1) | collective-permute-done | bytes 2097184 | tf_op jit(solution)/shard_map/ppermute | solution.py:16
  253.7 1.9 collective-permute-done
  257.8 1.8 slice_convert_fusion.6
  259.6 3.7 slice_convert_fusion
  263.3 35.8 %add_reduce_fusion.9 = (f32[16,16,1024]{2,1,0:T(8,128)}, f32[16,16,1024]{2,1,0:T(8,128)}, f32[16,16,1024]{2,1,0:T(8,128)}, f32[16,16,1024]{2,1,0:T(8,128)}, f32[16,16,1024]{2,1,0:T(8,128)}, /*index=5*/f32[16,16,1024]{2,1,0:T(8,128)}) fusion(f32[32,16,1024]{2,1,0:T(8,128)} %get-tuple-element.50, f32[32,16,1024]{2,1,0:T(8,128)} %get-tuple-element.48, ...), kind=kLoop, calls=%fused_computation.19 | loop fusion | flops 199753728 | bytes 23068672 | tf_op jit(solution)/shard_map/reduce_sum | solution.py:56
  299.1 1.8 maximum_multiply_fusion.1
  302.1 3.4 maximum_multiply_fusion
  313.0 164.2 %all-reduce.4.cloned.1.call-done = f32[3,16,16,2048]{3,2,1,0:T(8,128)} async-done(((f32[3,16,16,2048]{3,2,1,0:T(8,128)}), f32[3,16,16,2048]{3,2,1,0:T(8,128)}) %all-reduce.4.cloned.1.call-update) | async-done | bytes 6291472 | tf_op jit(solution)/shard_map/psum | solution.py:124
  477.2 6.4 fusion.1
  488.2 70.5 %subtract_reduce_fusion.2 = (bf16[32,16,1024]{2,1,0:T(8,128)(2,1)S(1)}, bf16[32,16,1024]{2,1,0:T(8,128)(2,1)S(1)}, f32[32,16,1024]{2,1,0:T(8,128)S(1)}, f32[32,1...) fusion(f32[16,16,1024]{2,1,0:T(8,128)S(1)} %get-tuple-element.5, ...), kind=kLoop, calls=%fused_computation.5 | loop fusion | flops 264241152 | bytes 23068672 | tf_op jit(solution)/shard_map/reduce_sum | solution.py:80
  558.7 1.9 pad_maximum_fusion.5
  560.6 6.5 collective-permute-start.5
  567.3 3.0 collective-permute-start.4
  570.3 1.5 pad_maximum_fusion.3
  571.7 1.9 collective-permute-start.3
  573.7 20.6 %add_reduce_fusion.4 = (f32[32,16,1024]{2,1,0:T(8,128)S(1)}, f32[32,16,1024]{2,1,0:T(8,128)S(1)}) fusion(f32[16,16,1024]{2,1,0:T(8,128)S(1)} %get-tuple-element.60, f32[16,16,1024]{2,1,0:T(8,128)S(1)} %get-tuple-element.59, f32[32,16,1024]{2,1,0:T(8,128)S(1)} %copy-done.9, f32[32,16,1024]{2,1,0:T(8,128)S(1)} %copy-done.10), kind=kLoop, calls=%fused_computation.9 | loop fusion | flops 66060288 | bytes 10485760 | tf_op jit(solution)/shard_map/reduce_sum | solution.py:68
  594.3 20.6 %add_reduce_fusion.5 = (f32[32,16,1024]{2,1,0:T(8,128)S(1)}, f32[32,16,1024]{2,1,0:T(8,128)S(1)}) fusion(f32[16,16,1024]{2,1,0:T(8,128)S(1)} %get-tuple-element.62, f32[16,16,1024]{2,1,0:T(8,128)S(1)} %get-tuple-element.61, f32[32,16,1024]{2,1,0:T(8,128)S(1)} %copy-done.8, f32[32,16,1024]{2,1,0:T(8,128)S(1)} %copy-done.7), kind=kLoop, calls=%fused_computation.11 | loop fusion | flops 66060288 | bytes 10485760 | tf_op jit(solution)/shard_map/reduce_sum | solution.py:68
  616.5 20.5 %add_reduce_fusion.6 = (f32[32,16,1024]{2,1,0:T(8,128)S(1)}, f32[32,16,1024]{2,1,0:T(8,128)S(1)}) fusion(f32[16,16,1024]{2,1,0:T(8,128)S(1)} %get-tuple-element.64, f32[16,16,1024]{2,1,0:T(8,128)S(1)} %get-tuple-element.63, f32[32,16,1024]{2,1,0:T(8,128)S(1)} %copy-done.4, f32[32,16,1024]{2,1,0:T(8,128)S(1)} %get-tuple-element.49), kind=kLoop, calls=%fused_computation.13 | loop fusion | flops 66060288 | bytes 10485760 | tf_op jit(solution)/shard_map/reduce_sum | solution.py:68
  637.1 17.6 %collective-permute-done.4 = bf16[32,16,2048]{2,1,0:T(8,128)(2,1)} collective-permute-done((bf16[32,16,2048]{2,1,0:T(8,128)(2,1)S(1)}, bf16[32,16,2048]{2,1,0:T(8,128)(2,1)}, u32[]{:S(2)}, u32[]{:S(2)}) %collective-permute-start.4) | collective-permute-done | bytes 2097184 | tf_op jit(solution)/shard_map/ppermute | solution.py:16
  654.6 22.6 %collective-permute-done.3 = bf16[32,16,2048]{2,1,0:T(8,128)(2,1)} collective-permute-done((bf16[32,16,2048]{2,1,0:T(8,128)(2,1)}, bf16[32,16,2048]{2,1,0:T(8,128)(2,1)}, u32[]{:S(2)}, u32[]{:S(2)}) %collective-permute-start.3) | collective-permute-done | bytes 2097184 | tf_op jit(solution)/shard_map/ppermute | solution.py:16
  677.2 5.7 fusion.25
  682.9 8.8 %all-to-all-start.1 = ((bf16[32,16,2048]{2,1,0:T(8,128)(2,1)}), bf16[32,16,2048]{2,1,0:T(8,128)(2,1)S(1)}, u32[]{:S(2)}, u32[]{:S(2)}) async-start(bf16[32,16,2048]{2,1,0:T(8,128)(2,1)} %fusion.25), calls=%async_computation.1 | async-start | bytes 4194304 | tf_op jit(solution)/shard_map/all_to_all | solution.py:141
  691.7 2.1 dynamic-slice_bitcast_fusion.3
  693.8 25.7 %all-to-all-done.1 = bf16[32,16,2048]{2,1,0:T(8,128)(2,1)S(1)} async-done(((bf16[32,16,2048]{2,1,0:T(8,128)(2,1)}), bf16[32,16,2048]{2,1,0:T(8,128)(2,1)S(1)}, u32[]{:S(2)}, u32[]{:S(2)}) %all-to-all-start.1) | async-done | bytes 2097184 | tf_op jit(solution)/shard_map/all_to_all | solution.py:141
  719.4 2.5 bitcast_convert_fusion
  721.9 5.5 copy.15
  727.4 3.5 fusion.39
  731.8 2.9 bitcast_multiply_fusion.1
  737.3 17.7 %fusion.49 = f32[512,2048]{1,0:T(8,128)S(1)} fusion(s32[512]{0:T(512)S(1)} %add_select_fusion.5, pred[512]{0:T(512)(128)(4,1)S(1)} %fusion.61, bf16[512,2048]{0,1:T(8,128)(2,1)S(1)} %fusion.40), kind=kOutput, calls=%fused_computation.107 | convolution fusion | flops 1091567616 | bytes 4721152 | tf_op jit(solution)/shard_map/dot_general | solution.py:150
  755.0 17.8 %fusion.50 = f32[512,2048]{1,0:T(8,128)S(1)} fusion(s32[512]{0:T(512)S(1)} %add_select_fusion.6, pred[512]{0:T(512)(128)(4,1)S(1)} %fusion.62, bf16[512,2048]{0,1:T(8,128)(2,1)S(1)} %fusion.40), kind=kOutput, calls=%fused_computation.108 | convolution fusion | flops 1091567616 | bytes 4721152 | tf_op jit(solution)/shard_map/dot_general | solution.py:150
  772.8 18.1 %fusion.51 = f32[512,2048]{1,0:T(8,128)S(1)} fusion(s32[512]{0:T(512)S(1)} %add_select_fusion.7, pred[512]{0:T(512)(128)(4,1)S(1)} %iota_compare_fusion, bf16[512,2048]{0,1:T(8,128)(2,1)S(1)} %fusion.40), kind=kOutput, calls=%fused_computation.109 | convolution fusion | flops 1091567616 | bytes 4721152 | tf_op jit(solution)/shard_map/dot_general | solution.py:150
  791.0 19.0 %fusion.38 = bf16[1,512,2048]{2,1,0:T(8,128)(2,1)} fusion(f32[512,2048]{1,0:T(8,128)S(1)} %fusion.49, f32[512,2048]{1,0:T(8,128)S(1)} %fusion.51, f32[512,2048]{1,0:T(8,128)S(1)} %fusion.50, s32[512]{0:T(512)S(1)} %add_select_fusion.4, pred[512]{0:T(512)(128)(4,1)S(1)} %fusion.60, bf16[512,2048]{0,1:T(8,128)(2,1)S(1)} %fusion.40), kind=kOutput, calls=%fused_computation.84 | convolution fusion | flops 1095761920 | bytes 15206912 | tf_op jit(solution)/shard_map/dot_general | solution.py:150
  (90 shorter events, 19.3 us)
Async XLA Ops:
  7.2 1.6 copy-start
  7.2 470.0 %all-reduce.4.cloned.1.call-start = ((), (), s32[]{:S(2)}) async-start(), calls=%async_computation.2 | async-start | bytes 12582912 | tf_op jit(solution)/shard_map/psum | solution.py:124
  43.4 34.8 %copy-start.13 = (f32[512,512]{1,0:T(8,128)}, f32[512,512]{1,0:T(8,128)S(1)}, u32[]{:S(2)}) copy-start(f32[512,512]{1,0:T(8,128)S(1)} %fusion.43) | copy-start | bytes 3145732
  61.0 17.2 %copy-start.15 = (f32[512,512]{1,0:T(8,128)}, f32[512,512]{1,0:T(8,128)S(1)}, u32[]{:S(2)}) copy-start(f32[512,512]{1,0:T(8,128)S(1)} %fusion.45) | copy-start | bytes 3145732
  78.2 1.0 copy-start.17
  79.2 2.0 copy-start.3
  82.6 3.9 copy-start.5
  157.6 8.4 %copy-start.25 = (s32[1,3]{1,0:T(1,128)S(1)}, s32[1,3]{1,0:T(1,128)}, u32[]{:S(2)}) copy-start(s32[1,3]{1,0:T(1,128)} %param.4) | copy-start | bytes 40
  161.1 28.9 %collective-permute-start.2 = (bf16[32,16,2048]{2,1,0:T(8,128)(2,1)S(1)}, bf16[32,16,2048]{2,1,0:T(8,128)(2,1)S(1)}, u32[]{:S(2)}, u32[]{:S(2)}) collective-permute-start(bf16[32,16,2048]{2,1,0:T(8,128)(2,1)S(1)} %bitcast.111), channel_id=1, source_target_pairs={{24,0},{32,8},{40,16},{48,24},{56,32},{64,40},{72,48},{80,56},{88,... | collective-permute-start | bytes 6291464 | tf_op jit(solution)/shard_map/ppermute | solution.py:16
  162.4 91.2 %collective-permute-start.1 = (bf16[32,16,2048]{2,1,0:T(8,128)(2,1)S(1)}, bf16[32,16,2048]{2,1,0:T(8,128)(2,1)S(1)}, u32[]{:S(2)}, u32[]{:S(2)}) collective-permute-start(bf16[32,16,2048]{2,1,0:T(8,128)(2,1)S(1)} %bitcast.112), channel_id=1, source_target_pairs={{16,0},{24,8},{32,16},{40,24},{48,32},{56,40},{64,48},{72,56},{80,... | collective-permute-start | bytes 6291464 | tf_op jit(solution)/shard_map/ppermute | solution.py:16
  163.7 91.9 %collective-permute-start = (bf16[32,16,2048]{2,1,0:T(8,128)(2,1)S(1)}, bf16[32,16,2048]{2,1,0:T(8,128)(2,1)S(1)}, u32[]{:S(2)}, u32[]{:S(2)}) collective-permute-start(bf16[32,16,2048]{2,1,0:T(8,128)(2,1)S(1)} %bitcast.113), channel_id=1, source_target_pairs={{8,0},{16,8},{24,16},{32,24},{40,32},{48,40},{56,48},{64,56},{72,6... | collective-permute-start | bytes 6291464 | tf_op jit(solution)/shard_map/ppermute | solution.py:16
  299.1 1.9 copy-start.23
  299.1 2.2 copy-start.24
  299.1 2.5 copy-start.21
  299.1 2.8 copy-start.22
  486.0 1.6 copy-start.11
  486.0 2.2 copy-start.12
  558.7 8.4 %copy-start.19 = (bf16[32,16,1024]{2,1,0:T(8,128)(2,1)S(1)}, bf16[32,16,1024]{2,1,0:T(8,128)(2,1)}, u32[]{:S(2)}) copy-start(bf16[32,16,1024]{2,1,0:T(8,128)(2,1)} %get-tuple-element.24) | copy-start | bytes 3145732
  558.7 8.4 %copy-start.20 = (bf16[32,16,1024]{2,1,0:T(8,128)(2,1)S(1)}, bf16[32,16,1024]{2,1,0:T(8,128)(2,1)}, u32[]{:S(2)}) copy-start(bf16[32,16,1024]{2,1,0:T(8,128)(2,1)} %get-tuple-element.25) | copy-start | bytes 3145732
  560.6 76.5 %collective-permute-start.5 = (bf16[32,16,2048]{2,1,0:T(8,128)(2,1)S(1)}, bf16[32,16,2048]{2,1,0:T(8,128)(2,1)}, u32[]{:S(2)}, u32[]{:S(2)}) collective-permute-start(bf16[32,16,2048]{2,1,0:T(8,128)(2,1)S(1)} %pad_maximum_fusion.5), channel_id=1, source_target_pairs={{0,24},{8,32},{16,40},{24,48},{32,56},{40,64},{48,72},{56,80},{64,... | collective-permute-start | bytes 6291464 | tf_op jit(solution)/shard_map/ppermute | solution.py:16
  567.1 6.6 copy-start.9
  567.1 6.6 copy-start.10
  567.3 87.3 %collective-permute-start.4 = (bf16[32,16,2048]{2,1,0:T(8,128)(2,1)S(1)}, bf16[32,16,2048]{2,1,0:T(8,128)(2,1)}, u32[]{:S(2)}, u32[]{:S(2)}) collective-permute-start(bf16[32,16,2048]{2,1,0:T(8,128)(2,1)S(1)} %pad_maximum_fusion.4), channel_id=1, source_target_pairs={{0,16},{8,24},{16,32},{24,40},{32,48},{40,56},{48,64},{56,72},{64,... | collective-permute-start | bytes 6291464 | tf_op jit(solution)/shard_map/ppermute | solution.py:16
  571.7 105.5 %collective-permute-start.3 = (bf16[32,16,2048]{2,1,0:T(8,128)(2,1)}, bf16[32,16,2048]{2,1,0:T(8,128)(2,1)}, u32[]{:S(2)}, u32[]{:S(2)}) collective-permute-start(bf16[32,16,2048]{2,1,0:T(8,128)(2,1)} %pad_maximum_fusion.3), channel_id=1, source_target_pairs={{0,8},{8,16},{16,24},{24,32},{32,40},{40,48},{48,56},{56,64},{64,7... | collective-permute-start | bytes 6291464 | tf_op jit(solution)/shard_map/ppermute | solution.py:16
  573.7 20.6 %copy-start.7 = (f32[32,16,1024]{2,1,0:T(8,128)S(1)}, f32[32,16,1024]{2,1,0:T(8,128)}, u32[]{:S(2)}) copy-start(f32[32,16,1024]{2,1,0:T(8,128)} %get-tuple-element.68) | copy-start | bytes 6291460
  573.7 20.6 %copy-start.8 = (f32[32,16,1024]{2,1,0:T(8,128)S(1)}, f32[32,16,1024]{2,1,0:T(8,128)}, u32[]{:S(2)}) copy-start(f32[32,16,1024]{2,1,0:T(8,128)} %get-tuple-element.69) | copy-start | bytes 6291460
  594.3 20.6 %copy-start.18 = (bf16[16,16,2048]{2,1,0:T(8,128)(2,1)S(1)}, bf16[16,16,2048]{2,1,0:T(8,128)(2,1)}, u32[]{:S(2)}) copy-start(bf16[16,16,2048]{2,1,0:T(8,128)(2,1)} %get-tuple-element.42) | copy-start | bytes 3145732
  614.9 1.6 copy-start.4
  682.9 36.5 %all-to-all-start.1 = ((bf16[32,16,2048]{2,1,0:T(8,128)(2,1)}), bf16[32,16,2048]{2,1,0:T(8,128)(2,1)S(1)}, u32[]{:S(2)}, u32[]{:S(2)}) async-start(bf16[32,16,2048]{2,1,0:T(8,128)(2,1)} %fusion.25), calls=%async_computation.1 | async-start | bytes 4194304 | tf_op jit(solution)/shard_map/all_to_all | solution.py:141
  721.9 5.5 copy-start.14
  721.9 5.5 copy-start.16
  731.7 3.5 copy-start.2
  731.8 4.1 copy-start.6
  790.9 19.0 %copy-start.1 = (bf16[1,512,2048]{2,1,0:T(8,128)(2,1)S(1)}, bf16[1,512,2048]{2,1,0:T(8,128)(2,1)}, u32[]{:S(2)}) copy-start(bf16[1,512,2048]{2,1,0:T(8,128)(2,1)} %param.3) | copy-start | bytes 6291460
Sparse Core Ops, SparseCore 0:
  305.7 171.4 all-reduce.3
where the time goes:
time: 826 us; the launch traced here: 817 us
  waiting for transfers between devices  315 us (38%)
  other arithmetic  230 us (28%)
  matrix products  142 us (17%)
  local copies, waits for them, and re-layouts  43.9 us (5%)
  blocking collectives  37 us (4%)
  starting transfers between devices  25.1 us (3%)
  between operations  24.1 us (3%)
    psum x1, waiting for transfers between devices, on_device(): totals = lax.psum(correl, 'grp')  164 us
    ppermute x6, waiting for transfers between devices, passed_along(): return lax.ppermute(array, axis, pairs)  125 us
    dot_general x4, matrix products, on_device(): jnp.dot(flat_grad[:, start_col:start_col + column_step], tables[table_ind...  72.6 us
    reduce_sum x1, other arithmetic, pull_second(): real_part = jnp.sum(left_real * right_real - left_imag * right_imag, axis=1)  70.5 us
    dot_general x4, matrix products, on_device(): jnp.dot(flat_traces, table_part, preferred_element_type=jnp.float32)  69.4 us
    reduce_sum x3, other arithmetic, pull_first(): real_part = jnp.sum(left_real * right_real + left_imag * right_imag, axis=2)  61.7 us
    all_to_all x1, blocking collectives, on_device(): lax.all_to_all(whitened, 'win', split_axis=1, concat_axis=0, tiled=True)  37 us
    reduce_sum x1, other arithmetic, correlate(): real_sum = jnp.sum(left_real * right_real + left_imag * right_imag, axis=0)  35.8 us
  transfers between devices with their start and end apart: 8, of which 7 were waited for; matrix products, arithmetic and copies ran while one was open for 8% of the time, Pallas kernels for 0%

commit v1 on v0

--- a/solution.py
+++ b/solution.py
@@ -1,3 +1,4 @@
+import functools
 import math
 import jax
 import jax.numpy as jnp
@@ -8,6 +9,19 @@
 FREQ = 1024
 BAND = 64
 OFFSETS = 4
+
+
+def bring_ends(q_in, axis_key):
+    opened = q_in
+    n_all = lax.axis_size(axis_key)
+    for c in [u for u in (1, 2, 4, 8, 16) if u < n_all]:
+        u1 = tuple(((w, w ^ c) for w in range(n_all)))
+        d_next = lax.ppermute(opened, axis_key, u1)
+        opened = opened + d_next
+    return opened
+
+
+serve_waves_all = functools.partial(bring_ends, axis_key="grp")
 
 
 def passed_along(array, axis, by):
@@ -121,7 +135,7 @@
         * live_slots
     )
     share_start = lax.axis_index("grp") * share_width
-    totals = lax.psum(correl, "grp")
+    totals = serve_waves_all(correl)
     correl_share = lax.dynamic_slice_in_dim(totals, share_start, share_width, 3)
     residual = ((totals - observed[0]) * live_slots).astype(jnp.bfloat16)
     own_grad = pull_first(residual[0], partners[0])

time: 826 us -> 1430 us (1.73)
  waiting for transfers between devices: 315 us -> 653 us
  starting transfers between devices: 25.1 us -> 290 us
    ppermute x0 -> x3, waiting for transfers between devices: none -> 522 us  [bring_ends(): d_next = lax.ppermute(opened, axis_key, u1)]
    ppermute x0 -> x3, starting transfers between devices: none -> 212 us  [bring_ends(): d_next = lax.ppermute(opened, axis_key, u1)]
    psum x1 -> x0, waiting for transfers between devices: 164 us -> none  [on_device(): totals = lax.psum(correl, 'grp')]
    ppermute x6, starting transfers between devices: 16.3 us -> 73.4 us  [passed_along(): return lax.ppermute(array, axis, pairs)]
    ppermute x6, waiting for transfers between devices: 125 us -> 106 us  [passed_along(): return lax.ppermute(array, axis, pairs)]
  transfers between devices with their start and end apart: 8 -> 10, of which waited for: 7 -> 8; matrix products, arithmetic and copies ran while one was open for 8% -> 5% of each run, Pallas kernels for 0% -> 0%
where the time goes in v1:
time: 1430 us; the launch traced here: 1420 us
  waiting for transfers between devices  653 us (46%)
  starting transfers between devices  290 us (20%)
  other arithmetic  243 us (17%)
  matrix products  142 us (10%)
  local copies, waits for them, and re-layouts  41.7 us (3%)
  blocking collectives  37 us (3%)
    ppermute x3, waiting for transfers between devices, bring_ends(): d_next = lax.ppermute(opened, axis_key, u1)  522 us
    ppermute x3, starting transfers between devices, bring_ends(): d_next = lax.ppermute(opened, axis_key, u1)  212 us
    ppermute x6, waiting for transfers between devices, passed_along(): return lax.ppermute(array, axis, pairs)  106 us
    ppermute x6, starting transfers between devices, passed_along(): return lax.ppermute(array, axis, pairs)  73.4 us
    dot_general x4, matrix products, on_device(): jnp.dot(flat_grad[:, start_col:start_col + column_step], tables[table_ind...  72.6 us
    reduce_sum x1, other arithmetic, pull_second(): real_part = jnp.sum(left_real * right_real - left_imag * right_imag, axis=1)  69.7 us
    dot_general x4, matrix products, on_device(): jnp.dot(flat_traces, table_part, preferred_element_type=jnp.float32)  69.4 us
    reduce_sum x3, other arithmetic, pull_first(): real_part = jnp.sum(left_real * right_real + left_imag * right_imag, axis=2)  61.8 us
  transfers between devices with their start and end apart: 10, of which 8 were waited for; matrix products, arithmetic and copies ran while one was open for 5% of the time, Pallas kernels for 0%

profile of v1, /device:TPU:1, one launch (start us, length us, event | category | flops | bytes accessed | tf_op | source)
XLA Modules:
  0.0 1418.1 jit_solution(4561760752926825286)
XLA Ops:
  2.2 17.5 %fusion.41 = f32[512,512]{1,0:T(8,128)S(1)} fusion(bf16[1,512,2048]{2,1,0:T(8,128)(2,1)S(1)} %copy-done, s32[512]{0:T(512)S(1)} %add_select_fusion.4, pred[512]{0:T(512)(128)(4,1)S(1)} %fusion.60), kind=kOutput, calls=%fused_computation.95 | convolution fusion | flops 1091567616 | bytes 3148288 | tf_op jit(solution)/shard_map/dot_general | solution.py:109
  19.7 17.2 %fusion.43 = f32[512,512]{1,0:T(8,128)S(1)} fusion(bf16[1,512,2048]{2,1,0:T(8,128)(2,1)S(1)} %copy-done, s32[512]{0:T(512)S(1)} %add_select_fusion.5, pred[512]{0:T(512)(128)(4,1)S(1)} %fusion.61), kind=kOutput, calls=%fused_computation.97 | convolution fusion | flops 1091567616 | bytes 3148288 | tf_op jit(solution)/shard_map/dot_general | solution.py:109
  36.9 17.6 %fusion.45 = f32[512,512]{1,0:T(8,128)S(1)} fusion(bf16[1,512,2048]{2,1,0:T(8,128)(2,1)S(1)} %copy-done, s32[512]{0:T(512)S(1)} %add_select_fusion.6, pred[512]{0:T(512)(128)(4,1)S(1)} %fusion.62), kind=kOutput, calls=%fused_computation.99 | convolution fusion | flops 1091567616 | bytes 3148288 | tf_op jit(solution)/shard_map/dot_general | solution.py:109
  54.6 17.2 %fusion.47 = f32[512,512]{1,0:T(8,128)S(1)} fusion(bf16[1,512,2048]{2,1,0:T(8,128)(2,1)S(1)} %copy-done, s32[512]{0:T(512)S(1)} %add_select_fusion.7, pred[512]{0:T(512)(128)(4,1)S(1)} %iota_compare_fusion), kind=kOutput, calls=%fused_computation.101 | convolution fusion | flops 1091567616 | bytes 3148288 | tf_op jit(solution)/shard_map/dot_general | solution.py:109
  71.8 2.4 maximum_bitcast_fusion
  74.2 4.4 multiply_add_fusion
  78.6 1.9 reduce_sum.206
  82.1 2.8 fusion.16
  84.9 10.8 copy.14
  96.3 13.2 reduce.2
  109.4 2.8 reshape.499
  112.2 37.0 %all_to_all.21 = bf16[32,2,16384]{2,1,0:T(2,128)(2,1)S(1)} all-to-all(bf16[32,2,16384]{2,1,0:T(2,128)(2,1)} %reshape.499), channel_id=1, replica_groups=mesh['win'=32,'grp'=8] {'win'}, dimensions={0} | all-to-all | bytes 4194304 | tf_op jit(solution)/shard_map/all_to_all | solution.py:118
  149.2 6.8 reshape.500
  155.9 3.5 copy.17
  162.0 2.7 collective-permute-start
  167.4 2.4 slice_convert_fusion.7
  169.8 18.5 %collective-permute-done.2 = bf16[32,16,2048]{2,1,0:T(8,128)(2,1)S(1)} collective-permute-done((bf16[32,16,2048]{2,1,0:T(8,128)(2,1)S(1)}, bf16[32,16,2048]{2,1,0:T(8,128)(2,1)S(1)}, u32[]{:S(2)}, u32[]{:S(2)}) %collective-permute-start.2) | collective-permute-done | bytes 2097184 | tf_op jit(solution)/shard_map/ppermute | solution.py:30
  188.3 63.7 %collective-permute-done.1 = bf16[32,16,2048]{2,1,0:T(8,128)(2,1)S(1)} collective-permute-done((bf16[32,16,2048]{2,1,0:T(8,128)(2,1)S(1)}, bf16[32,16,2048]{2,1,0:T(8,128)(2,1)S(1)}, u32[]{:S(2)}, u32[]{:S(2)}) %collective-permute-start.1) | collective-permute-done | bytes 2097184 | tf_op jit(solution)/shard_map/ppermute | solution.py:30
  252.0 1.9 collective-permute-done
  257.9 3.9 slice_convert_fusion
  261.8 35.3 %add_reduce_fusion.9 = (f32[16,16,1024]{2,1,0:T(8,128)S(1)}, f32[16,16,1024]{2,1,0:T(8,128)}, f32[16,16,1024]{2,1,0:T(8,128)}, f32[16,16,1024]{2,1,0:T(8,128)}, ...) fusion(f32[32,16,1024]{2,1,0:T(8,128)} %get-tuple-element.52, f32[32,16,1024]{2,1,0:T(8,128)} %get-tuple-element.50, ...), kind=kLoop, calls=%fused_computation.19 | loop fusion | flops 199753728 | bytes 23068672 | tf_op jit(solution)/shard_map/reduce_sum | solution.py:70
  302.7 131.5 %collective-permute-done.3 = f32[3,16,16,2048]{3,2,1,0:T(8,128)S(1)} collective-permute-done((f32[3,16,16,2048]{3,2,1,0:T(8,128)S(1)}, f32[3,16,16,2048]{3,2,1,0:T(8,128)S(1)}, u32[]{:S(2)}, u32[]{:S(2)}) %collective-permute-start.3) | collective-permute-done | bytes 6291488 | tf_op jit(solution)/shard_map/ppermute | solution.py:19
  435.4 2.7 collective-permute-start.4
  438.1 261.3 %collective-permute-done.4 = f32[3,16,16,2048]{3,2,1,0:T(8,128)S(1)} collective-permute-done((f32[3,16,16,2048]{3,2,1,0:T(8,128)S(1)}, f32[3,16,16,2048]{3,2,1,0:T(8,128)S(1)}, u32[]{:S(2)}, u32[]{:S(2)}) %collective-permute-start.4) | collective-permute-done | bytes 6291488 | tf_op jit(solution)/shard_map/ppermute | solution.py:19
  699.4 3.7 fusion.101
  703.1 207.4 %collective-permute-start.5 = (f32[3,16,16,2048]{3,2,1,0:T(8,128)}, f32[3,16,16,2048]{3,2,1,0:T(8,128)}, u32[]{:S(2)}, u32[]{:S(2)}) collective-permute-start(f32[3,16,16,2048]{3,2,1,0:T(8,128)} %fusion.101), channel_id=1, source_target_pairs={{0,4},{1,5},{2,6},{3,7},{4,0},{5,1},{6,2},{7,3},{8,12},{9,13},{10,... | collective-permute-start | bytes 18874376 | tf_op jit(solution)/shard_map/ppermute | solution.py:19
  918.2 129.2 %collective-permute-done.5 = f32[3,16,16,2048]{3,2,1,0:T(8,128)} collective-permute-done((f32[3,16,16,2048]{3,2,1,0:T(8,128)}, f32[3,16,16,2048]{3,2,1,0:T(8,128)}, u32[]{:S(2)}, u32[]{:S(2)}) %collective-permute-start.5) | collective-permute-done | bytes 6291488 | tf_op jit(solution)/shard_map/ppermute | solution.py:19
  1047.5 12.3 fusion.1
  1063.7 69.7 %subtract_reduce_fusion.2 = (bf16[32,16,1024]{2,1,0:T(8,128)(2,1)S(1)}, bf16[32,16,1024]{2,1,0:T(8,128)(2,1)S(1)}, f32[32,16,1024]{2,1,0:T(8,128)S(1)}, f32[32,1...) fusion(f32[16,16,1024]{2,1,0:T(8,128)S(1)} %get-tuple-element.6, ...), kind=kLoop, calls=%fused_computation.5 | loop fusion | flops 264241152 | bytes 23068672 | tf_op jit(solution)/shard_map/reduce_sum | solution.py:94
  1134.8 2.6 collective-permute-start.8
  1137.7 63.4 %collective-permute-start.7 = (bf16[32,16,2048]{2,1,0:T(8,128)(2,1)S(1)}, bf16[32,16,2048]{2,1,0:T(8,128)(2,1)S(1)}, u32[]{:S(2)}, u32[]{:S(2)}) collective-permute-start(bf16[32,16,2048]{2,1,0:T(8,128)(2,1)S(1)} %pad_maximum_fusion.4), channel_id=1, source_target_pairs={{0,16},{8,24},{16,32},{24,40},{32,48},{40,56},{48,64},{56,72},{64,... | collective-permute-start | bytes 6291464 | tf_op jit(solution)/shard_map/ppermute | solution.py:30
  1202.5 2.1 collective-permute-start.6
  1204.7 20.6 %add_reduce_fusion.6 = (f32[32,16,1024]{2,1,0:T(8,128)S(1)}, f32[32,16,1024]{2,1,0:T(8,128)S(1)}) fusion(f32[16,16,1024]{2,1,0:T(8,128)S(1)} %get-tuple-element.66, f32[16,16,1024]{2,1,0:T(8,128)S(1)} %get-tuple-element.65, f32[32,16,1024]{2,1,0:T(8,128)S(1)} %copy-done.5, f32[32,16,1024]{2,1,0:T(8,128)S(1)} %copy-done.4), kind=kLoop, calls=%fused_computation.13 | loop fusion | flops 66060288 | bytes 10485760 | tf_op jit(solution)/shard_map/reduce_sum | solution.py:82
  1225.3 20.6 %add_reduce_fusion.5 = (f32[32,16,1024]{2,1,0:T(8,128)S(1)}, f32[32,16,1024]{2,1,0:T(8,128)S(1)}) fusion(f32[16,16,1024]{2,1,0:T(8,128)S(1)} %get-tuple-element.64, f32[16,16,1024]{2,1,0:T(8,128)S(1)} %get-tuple-element.63, f32[32,16,1024]{2,1,0:T(8,128)S(1)} %copy-done.11, f32[32,16,1024]{2,1,0:T(8,128)S(1)} %copy-done.10), kind=kLoop, calls=%fused_computation.11 | loop fusion | flops 66060288 | bytes 10485760 | tf_op jit(solution)/shard_map/reduce_sum | solution.py:82
  1247.5 20.6 %add_reduce_fusion.4 = (f32[32,16,1024]{2,1,0:T(8,128)S(1)}, f32[32,16,1024]{2,1,0:T(8,128)S(1)}) fusion(f32[16,16,1024]{2,1,0:T(8,128)S(1)} %get-tuple-element.62, f32[16,16,1024]{2,1,0:T(8,128)S(1)} %get-tuple-element.61, f32[32,16,1024]{2,1,0:T(8,128)S(1)} %copy-done.8, f32[32,16,1024]{2,1,0:T(8,128)S(1)} %copy-done.9), kind=kLoop, calls=%fused_computation.9 | loop fusion | flops 66060288 | bytes 10485760 | tf_op jit(solution)/shard_map/reduce_sum | solution.py:82
  1268.1 21.4 %collective-permute-done.6 = bf16[32,16,2048]{2,1,0:T(8,128)(2,1)} collective-permute-done((bf16[32,16,2048]{2,1,0:T(8,128)(2,1)}, bf16[32,16,2048]{2,1,0:T(8,128)(2,1)}, u32[]{:S(2)}, u32[]{:S(2)}) %collective-permute-start.6) | collective-permute-done | bytes 2097184 | tf_op jit(solution)/shard_map/ppermute | solution.py:30
  1289.6 5.3 fusion.25
  1294.8 4.3 all-to-all-start.1
  1299.2 2.1 dynamic-slice_bitcast_fusion.3
  1301.2 25.7 %all-to-all-done.1 = bf16[32,16,2048]{2,1,0:T(8,128)(2,1)S(1)} async-done(((bf16[32,16,2048]{2,1,0:T(8,128)(2,1)}), bf16[32,16,2048]{2,1,0:T(8,128)(2,1)S(1)}, u32[]{:S(2)}, u32[]{:S(2)}) %all-to-all-start.1) | async-done | bytes 2097184 | tf_op jit(solution)/shard_map/all_to_all | solution.py:155
  1327.0 2.5 bitcast_convert_fusion
  1329.5 5.5 copy.15
  1335.0 3.5 fusion.39
  1339.3 2.9 bitcast_multiply_fusion.1
  1345.2 17.7 %fusion.49 = f32[512,2048]{1,0:T(8,128)S(1)} fusion(s32[512]{0:T(512)S(1)} %add_select_fusion.5, pred[512]{0:T(512)(128)(4,1)S(1)} %copy-done.36, bf16[512,2048]{0,1:T(8,128)(2,1)S(1)} %fusion.40), kind=kOutput, calls=%fused_computation.107 | convolution fusion | flops 1091567616 | bytes 4721152 | tf_op jit(solution)/shard_map/dot_general | solution.py:164
  1363.0 17.8 %fusion.51 = f32[512,2048]{1,0:T(8,128)S(1)} fusion(s32[512]{0:T(512)S(1)} %copy-done.30, pred[512]{0:T(512)(128)(4,1)S(1)} %copy-done.38, bf16[512,2048]{0,1:T(8,128)(2,1)S(1)} %fusion.40), kind=kOutput, calls=%fused_computation.109 | convolution fusion | flops 1091567616 | bytes 4721152 | tf_op jit(solution)/shard_map/dot_general | solution.py:164
  1380.8 18.1 %fusion.50 = f32[512,2048]{1,0:T(8,128)S(1)} fusion(s32[512]{0:T(512)S(1)} %add_select_fusion.6, pred[512]{0:T(512)(128)(4,1)S(1)} %copy-done.34, bf16[512,2048]{0,1:T(8,128)(2,1)S(1)} %fusion.40), kind=kOutput, calls=%fused_computation.108 | convolution fusion | flops 1091567616 | bytes 4721152 | tf_op jit(solution)/shard_map/dot_general | solution.py:164
  1399.0 19.0 %fusion.38 = bf16[1,512,2048]{2,1,0:T(8,128)(2,1)} fusion(f32[512,2048]{1,0:T(8,128)S(1)} %fusion.49, f32[512,2048]{1,0:T(8,128)S(1)} %fusion.51, f32[512,2048]{1,0:T(8,128)S(1)} %fusion.50, s32[512]{0:T(512)S(1)} %copy-done.28, pred[512]{0:T(512)(128)(4,1)S(1)} %copy-done.32, bf16[512,2048]{0,1:T(8,128)(2,1)S(1)} %fusion.40), kind=kOutput, calls=%fused_computation.84 | convolution fusion | flops 1095761920 | bytes 15206912 | tf_op jit(solution)/shard_map/dot_general | solution.py:164
  (121 shorter events, 29.9 us)
Async XLA Ops:
  0.6 1.6 copy-start
  0.7 19.0 %copy-start.27 = (s32[512]{0:T(512)}, s32[512]{0:T(512)S(1)}, u32[]{:S(2)}) copy-start(s32[512]{0:T(512)S(1)} %add_select_fusion.4) | copy-start | bytes 6148
  0.7 19.0 %copy-start.31 = (pred[512]{0:T(512)(128)(4,1)}, pred[512]{0:T(512)(128)(4,1)S(1)}, u32[]{:S(2)}) copy-start(pred[512]{0:T(512)(128)(4,1)S(1)} %fusion.60) | copy-start | bytes 1540
  0.7 19.0 %copy-start.35 = (pred[512]{0:T(512)(128)(4,1)}, pred[512]{0:T(512)(128)(4,1)S(1)}, u32[]{:S(2)}) copy-start(pred[512]{0:T(512)(128)(4,1)S(1)} %fusion.61) | copy-start | bytes 1540
  0.7 36.2 %copy-start.33 = (pred[512]{0:T(512)(128)(4,1)}, pred[512]{0:T(512)(128)(4,1)S(1)}, u32[]{:S(2)}) copy-start(pred[512]{0:T(512)(128)(4,1)S(1)} %fusion.62) | copy-start | bytes 1540
  0.8 53.8 %copy-start.29 = (s32[512]{0:T(512)}, s32[512]{0:T(512)S(1)}, u32[]{:S(2)}) copy-start(s32[512]{0:T(512)S(1)} %add_select_fusion.7) | copy-start | bytes 6148
  2.2 52.3 %copy-start.37 = (pred[512]{0:T(512)(128)(4,1)}, pred[512]{0:T(512)(128)(4,1)S(1)}, u32[]{:S(2)}) copy-start(pred[512]{0:T(512)(128)(4,1)S(1)} %iota_compare_fusion) | copy-start | bytes 1540
  19.7 61.0 %copy-start.14 = (f32[512,512]{1,0:T(8,128)}, f32[512,512]{1,0:T(8,128)S(1)}, u32[]{:S(2)}) copy-start(f32[512,512]{1,0:T(8,128)S(1)} %fusion.41) | copy-start | bytes 3145732
  36.9 34.8 %copy-start.16 = (f32[512,512]{1,0:T(8,128)}, f32[512,512]{1,0:T(8,128)S(1)}, u32[]{:S(2)}) copy-start(f32[512,512]{1,0:T(8,128)S(1)} %fusion.43) | copy-start | bytes 3145732
  54.6 17.2 %copy-start.19 = (f32[512,512]{1,0:T(8,128)}, f32[512,512]{1,0:T(8,128)S(1)}, u32[]{:S(2)}) copy-start(f32[512,512]{1,0:T(8,128)S(1)} %fusion.45) | copy-start | bytes 3145732
  71.7 2.4 copy-start.22
  74.2 7.9 copy-start.17
  74.2 7.9 copy-start.20
  155.9 8.8 copy-start.26
  159.4 28.9 %collective-permute-start.2 = (bf16[32,16,2048]{2,1,0:T(8,128)(2,1)S(1)}, bf16[32,16,2048]{2,1,0:T(8,128)(2,1)S(1)}, u32[]{:S(2)}, u32[]{:S(2)}) collective-permute-start(bf16[32,16,2048]{2,1,0:T(8,128)(2,1)S(1)} %bitcast.111), channel_id=1, source_target_pairs={{24,0},{32,8},{40,16},{48,24},{56,32},{64,40},{72,48},{80,56},{88,... | collective-permute-start | bytes 6291464 | tf_op jit(solution)/shard_map/ppermute | solution.py:30
  160.7 91.2 %collective-permute-start.1 = (bf16[32,16,2048]{2,1,0:T(8,128)(2,1)S(1)}, bf16[32,16,2048]{2,1,0:T(8,128)(2,1)S(1)}, u32[]{:S(2)}, u32[]{:S(2)}) collective-permute-start(bf16[32,16,2048]{2,1,0:T(8,128)(2,1)S(1)} %bitcast.112), channel_id=1, source_target_pairs={{16,0},{24,8},{32,16},{40,24},{48,32},{56,40},{64,48},{72,56},{80,... | collective-permute-start | bytes 6291464 | tf_op jit(solution)/shard_map/ppermute | solution.py:30
  162.0 91.9 %collective-permute-start = (bf16[32,16,2048]{2,1,0:T(8,128)(2,1)S(1)}, bf16[32,16,2048]{2,1,0:T(8,128)(2,1)S(1)}, u32[]{:S(2)}, u32[]{:S(2)}) collective-permute-start(bf16[32,16,2048]{2,1,0:T(8,128)(2,1)S(1)} %bitcast.113), channel_id=1, source_target_pairs={{8,0},{16,8},{24,16},{32,24},{40,32},{48,40},{56,48},{64,56},{72,6... | collective-permute-start | bytes 6291464 | tf_op jit(solution)/shard_map/ppermute | solution.py:30
  257.9 3.9 copy-start.3
  297.1 1.9 copy-start.24
  297.1 2.2 copy-start.25
  297.1 2.5 copy-start.23
  301.0 133.2 %collective-permute-start.3 = (f32[3,16,16,2048]{3,2,1,0:T(8,128)S(1)}, f32[3,16,16,2048]{3,2,1,0:T(8,128)S(1)}, u32[]{:S(2)}, u32[]{:S(2)}) collective-permute-start(f32[3,16,16,2048]{3,2,1,0:T(8,128)S(1)} %maximum_multiply_fusion), channel_id=1, source_target_pairs={{0,1},{1,0},{2,3},{3,2},{4,5},{5,4},{6,7},{7,6},{8,9},{9,8},{10,11... | collective-permute-start | bytes 18874376 | tf_op jit(solution)/shard_map/ppermute | solution.py:19
  435.4 264.0 %collective-permute-start.4 = (f32[3,16,16,2048]{3,2,1,0:T(8,128)S(1)}, f32[3,16,16,2048]{3,2,1,0:T(8,128)S(1)}, u32[]{:S(2)}, u32[]{:S(2)}) collective-permute-start(f32[3,16,16,2048]{3,2,1,0:T(8,128)S(1)} %fusion.100), channel_id=1, source_target_pairs={{0,2},{1,3},{2,0},{3,1},{4,6},{5,7},{6,4},{7,5},{8,10},{9,11},{10,... | collective-permute-start | bytes 18874376 | tf_op jit(solution)/shard_map/ppermute | solution.py:19
  703.1 344.4 %collective-permute-start.5 = (f32[3,16,16,2048]{3,2,1,0:T(8,128)}, f32[3,16,16,2048]{3,2,1,0:T(8,128)}, u32[]{:S(2)}, u32[]{:S(2)}) collective-permute-start(f32[3,16,16,2048]{3,2,1,0:T(8,128)} %fusion.101), channel_id=1, source_target_pairs={{0,4},{1,5},{2,6},{3,7},{4,0},{5,1},{6,2},{7,3},{8,12},{9,13},{10,... | collective-permute-start | bytes 18874376 | tf_op jit(solution)/shard_map/ppermute | solution.py:19
  1061.5 1.6 copy-start.12
  1061.5 2.2 copy-start.13
  1134.8 133.3 %collective-permute-start.8 = (bf16[32,16,2048]{2,1,0:T(8,128)(2,1)S(1)}, bf16[32,16,2048]{2,1,0:T(8,128)(2,1)}, u32[]{:S(2)}, u32[]{:S(2)}) collective-permute-start(bf16[32,16,2048]{2,1,0:T(8,128)(2,1)S(1)} %pad_maximum_fusion.5), channel_id=1, source_target_pairs={{0,24},{8,32},{16,40},{24,48},{32,56},{40,64},{48,72},{56,80},{64,... | collective-permute-start | bytes 6291464 | tf_op jit(solution)/shard_map/ppermute | solution.py:30
  1137.5 67.2 %copy-start.4 = (f32[32,16,1024]{2,1,0:T(8,128)S(1)}, f32[32,16,1024]{2,1,0:T(8,128)}, u32[]{:S(2)}) copy-start(f32[32,16,1024]{2,1,0:T(8,128)} %copy-done.3) | copy-start | bytes 6291460
  1137.5 67.2 %copy-start.5 = (f32[32,16,1024]{2,1,0:T(8,128)S(1)}, f32[32,16,1024]{2,1,0:T(8,128)}, u32[]{:S(2)}) copy-start(f32[32,16,1024]{2,1,0:T(8,128)} %get-tuple-element.52) | copy-start | bytes 6291460
  1137.7 130.4 %collective-permute-start.7 = (bf16[32,16,2048]{2,1,0:T(8,128)(2,1)S(1)}, bf16[32,16,2048]{2,1,0:T(8,128)(2,1)S(1)}, u32[]{:S(2)}, u32[]{:S(2)}) collective-permute-start(bf16[32,16,2048]{2,1,0:T(8,128)(2,1)S(1)} %pad_maximum_fusion.4), channel_id=1, source_target_pairs={{0,16},{8,24},{16,32},{24,40},{32,48},{40,56},{48,64},{56,72},{64,... | collective-permute-start | bytes 6291464 | tf_op jit(solution)/shard_map/ppermute | solution.py:30
  1202.5 87.1 %collective-permute-start.6 = (bf16[32,16,2048]{2,1,0:T(8,128)(2,1)}, bf16[32,16,2048]{2,1,0:T(8,128)(2,1)}, u32[]{:S(2)}, u32[]{:S(2)}) collective-permute-start(bf16[32,16,2048]{2,1,0:T(8,128)(2,1)} %pad_maximum_fusion.3), channel_id=1, source_target_pairs={{0,8},{8,16},{16,24},{24,32},{32,40},{40,48},{48,56},{56,64},{64,7... | collective-permute-start | bytes 6291464 | tf_op jit(solution)/shard_map/ppermute | solution.py:30
  1204.7 20.6 %copy-start.10 = (f32[32,16,1024]{2,1,0:T(8,128)S(1)}, f32[32,16,1024]{2,1,0:T(8,128)}, u32[]{:S(2)}) copy-start(f32[32,16,1024]{2,1,0:T(8,128)} %get-tuple-element.70) | copy-start | bytes 6291460
  1204.7 20.6 %copy-start.11 = (f32[32,16,1024]{2,1,0:T(8,128)S(1)}, f32[32,16,1024]{2,1,0:T(8,128)}, u32[]{:S(2)}) copy-start(f32[32,16,1024]{2,1,0:T(8,128)} %get-tuple-element.71) | copy-start | bytes 6291460
  1225.3 20.9 %copy-start.9 = (f32[32,16,1024]{2,1,0:T(8,128)S(1)}, f32[32,16,1024]{2,1,0:T(8,128)}, u32[]{:S(2)}) copy-start(f32[32,16,1024]{2,1,0:T(8,128)} %get-tuple-element.46) | copy-start | bytes 6291460
  1245.9 1.6 copy-start.8
  1294.8 32.1 %all-to-all-start.1 = ((bf16[32,16,2048]{2,1,0:T(8,128)(2,1)}), bf16[32,16,2048]{2,1,0:T(8,128)(2,1)S(1)}, u32[]{:S(2)}, u32[]{:S(2)}) async-start(bf16[32,16,2048]{2,1,0:T(8,128)(2,1)} %fusion.25), calls=%async_computation.1 | async-start | bytes 4194304 | tf_op jit(solution)/shard_map/all_to_all | solution.py:155
  1329.5 5.5 copy-start.15
  1329.5 5.5 copy-start.18
  1329.5 5.5 copy-start.21
  1339.3 3.5 copy-start.2
  1339.3 4.1 copy-start.7
  1343.4 1.8 copy-start.36
  1345.2 17.8 %copy-start.30 = (s32[512]{0:T(512)S(1)}, s32[512]{0:T(512)}, u32[]{:S(2)}) copy-start(s32[512]{0:T(512)} %copy-done.29) | copy-start | bytes 6148
  1345.2 17.8 %copy-start.38 = (pred[512]{0:T(512)(128)(4,1)S(1)}, pred[512]{0:T(512)(128)(4,1)}, u32[]{:S(2)}) copy-start(pred[512]{0:T(512)(128)(4,1)} %copy-done.37) | copy-start | bytes 1540
  1363.0 17.8 %copy-start.34 = (pred[512]{0:T(512)(128)(4,1)S(1)}, pred[512]{0:T(512)(128)(4,1)}, u32[]{:S(2)}) copy-start(pred[512]{0:T(512)(128)(4,1)} %copy-done.33) | copy-start | bytes 1540
  1380.8 18.2 %copy-start.28 = (s32[512]{0:T(512)S(1)}, s32[512]{0:T(512)}, u32[]{:S(2)}) copy-start(s32[512]{0:T(512)} %copy-done.27) | copy-start | bytes 6148
  1380.8 18.2 %copy-start.32 = (pred[512]{0:T(512)(128)(4,1)S(1)}, pred[512]{0:T(512)(128)(4,1)}, u32[]{:S(2)}) copy-start(pred[512]{0:T(512)(128)(4,1)} %copy-done.31) | copy-start | bytes 1540
  1399.0 19.0 %copy-start.1 = (bf16[1,512,2048]{2,1,0:T(8,128)(2,1)S(1)}, bf16[1,512,2048]{2,1,0:T(8,128)(2,1)}, u32[]{:S(2)}) copy-start(bf16[1,512,2048]{2,1,0:T(8,128)(2,1)} %param.3) | copy-start | bytes 6291460
  (1 other events, 1.3 us)
